TPU v7x, 32 devices: a whole 2x2x4 slice. The times are simulated.
32 devices in a mesh: group: 4 (over x, core), shard: 8 (over z, y).
Axes of the slice: x: 2, y: 2, z: 4, core: 2. Of those that a mesh axis runs over, the one named last changes fastest.
Arguments:
- hidden: bfloat16 [8192, 768], P(('group', 'shard')), may hold values from -40 to 40
- out_grads: bfloat16 [5, 8192, 768], P(None, ('group', 'shard')), may hold values from -40 to 40
- global_inputs: bfloat16 [1024, 768], P(('group', 'shard')), may hold values from -40 to 40
- query_grads: bfloat16 [1024, 768], P(('group', 'shard')), may hold values from -40 to 40
- weight_grads: bfloat16 [6, 768, 768], P(None, 'shard'), may hold values from -48 to 48
- momentum: float32 [6, 768, 768], P(None, 'shard', 'group'), may hold values from -6 to 6
Outputs:
- new_momentum: float32 [6, 768, 768], P(None, 'shard', 'group')
All inputs are finite; a program needn't handle non-finite values. Where the computation divides by a largest or mean magnitude, that divisor is 1e-20 or more.
Results may differ from a plain program's by a relative error of at most 0.0018.
Values may be sent and summed in bfloat16 or wider, within the bound.
A program may use at most 128 MiB of HBM per device.

v0:
```python
import jax
import jax.numpy as jnp
from jax import lax
from jax.sharding import PartitionSpec as P

ITERS = 3
PRECISE = lax.Precision.HIGHEST
DAMPING = 0.1
MOMENTUM = 0.9


def broadcast(array, axis, root):
    mine = lax.axis_index(axis) == root
    return lax.psum(jnp.where(mine, array, jnp.zeros_like(array)), axis)


def outer_sum(matrix_rows):
    return lax.dot_general(
        matrix_rows, matrix_rows, (((0,), (0,)), ((), ())), preferred_element_type=jnp.float32
    )


def on_device(hidden, out_grads, global_inputs, query_grads, weight_grads, momentum):
    model_width = hidden.shape[1]
    group_size = lax.axis_size("group")
    shard_size = lax.axis_size("shard")
    per_group = 8 // group_size
    row_block = model_width // shard_size
    col_block = momentum.shape[2]
    shard_pos = lax.axis_index("shard")
    group_pos = lax.axis_index("group")
    devices = group_size * shard_size
    partials = [outer_sum(hidden), outer_sum(global_inputs)]
    partials = partials + [outer_sum(out_grads[member]) for member in range(5)]
    partials = partials + [outer_sum(query_grads)]
    stacked = jnp.stack([single.astype(jnp.bfloat16) for single in partials])
    summed = lax.psum_scatter(stacked, "group", scatter_dimension=0, tiled=True).astype(jnp.float32)
    factor_ids = group_pos * per_group + jnp.arange(per_group)
    is_global = (factor_ids == 1) | (factor_ids == 7)
    samp_total = float(hidden.shape[0] * devices)
    glob_total = float(global_inputs.shape[0] * devices)
    counted = jnp.where(is_global, glob_total, samp_total).astype(jnp.float32)
    factor_full = lax.psum(summed, "shard")
    covariance = factor_full / counted[:, None, None]
    mean_diag = jnp.trace(covariance, axis1=1, axis2=2) / model_width
    eye_full = jnp.eye(model_width, dtype=jnp.float32)
    matrix = covariance / mean_diag[:, None, None] + DAMPING * eye_full
    row_limit = jnp.max(jnp.sum(jnp.abs(matrix), axis=2), axis=1)
    approx = jnp.broadcast_to(eye_full, matrix.shape) / row_limit[:, None, None]
    for iteration in range(ITERS):
        product = jnp.einsum("kij,kjl->kil", matrix, approx, precision=PRECISE)
        approx = 2.0 * approx - jnp.einsum("kij,kjl->kil", approx, product, precision=PRECISE)
    own_rows = lax.dynamic_slice_in_dim(approx, shard_pos * row_block, row_block, 1)
    all_rows = lax.all_gather(own_rows, "group", axis=0, tiled=True)
    input_inv = jnp.stack(
        [broadcast(approx[factor % per_group], "group", factor // per_group) for factor in range(2)]
    )
    input_cols = lax.dynamic_slice_in_dim(input_inv, group_pos * col_block, col_block, 2)
    out_inverse = all_rows[2:8]
    initial = jnp.zeros(out_inverse.shape, jnp.float32)
    gathered = lax.all_gather(weight_grads, "shard", axis=1, tiled=True)
    columns = lax.slice_in_dim(out_inverse, 0, gathered.shape[1], axis=2)
    left_side = initial + jnp.einsum(
        "wrn,wnd->wrd", columns, gathered.astype(jnp.float32), precision=PRECISE
    )
    local_part = jnp.einsum("wrd,de->wre", left_side[0:5], input_cols[0], precision=PRECISE)
    global_part = jnp.dot(left_side[5], input_cols[1], precision=PRECISE)[None]
    return MOMENTUM * momentum + jnp.concatenate([local_part, global_part], axis=0)


def solution(mesh):
    placed = (
        P(("group", "shard"), None),
        P(None, ("group", "shard"), None),
        P(("group", "shard"), None),
        P(("group", "shard"), None),
        P(None, "shard", None),
        P(None, "shard", "group"),
    )
    return jax.shard_map(
        on_device, mesh=mesh, in_specs=placed, out_specs=P(None, "shard", "group"), check_vma=False
    )
```

profile of v0, /device:TPU:0, one launch (start us, length us, event | category | flops | bytes accessed | tf_op | source)
XLA Modules:
  0.0 529.7 jit_solution(5312361933273675997)
XLA Ops:
  9.9 2.4 fusion.10
  12.3 2.7 fusion.16
  15.0 1.6 fusion.18
  16.6 1.6 fusion.20
  18.1 1.6 fusion.22
  21.2 1.6 fusion.12
  23.3 1.5 fusion.26
  24.8 79.3 %reduce-scatter.2.cloned.1.call-done = bf16[2,768,768]{2,1,0:T(8,128)(2,1)} async-done(((bf16[8,768,768]{2,1,0:T(8,128)(2,1)}), bf16[2,768,768]{2,1,0:T(8,128)(2,1)}) %reduce-scatter.2.cloned.1.call-update) | async-done | bytes 2359312 | tf_op jit(solution)/shard_map/reduce_scatter | solution.py:37
  104.1 187.7 %all-reduce.5 = f32[2,768,768]{2,1,0:T(8,128)} all-reduce(bf16[2,768,768]{2,1,0:T(8,128)(2,1)} %reduce-scatter.2.cloned.1.call-done), channel_id=1, replica_groups=mesh['group'=4,'shard'=8] {'shard'}, use_global_device_ids=true, to_apply=%region_1.2 | all-reduce | flops 1179648 | bytes 7077888 | tf_op jit(solution)/shard_map/psum | solution.py:43
  291.9 3.7 select_reduce_fusion
  295.6 3.0 abs_reduce_fusion
  298.7 15.6 %fusion.2 = f32[2,768,768]{2,1,0:T(8,128)S(1)} fusion(f32[2,768,768]{2,1,0:T(8,128)} %get-tuple-element.8, f32[2]{0:T(128)S(1)} %reduce_max.9, f32[768,768]{1,0:T(8,128)} %fusion.26), kind=kOutput, calls=%fused_computation.10 | convolution fusion | flops 10872815616 | bytes 11796488 | tf_op jit(solution)/shard_map/kij,kjl->kil/dot_general | solution.py:51
  314.3 12.8 %multiply_subtract_fusion.2 = f32[2,768,768]{2,1,0:T(8,128)S(1)} fusion(f32[2]{0:T(128)S(1)} %reduce_max.9, f32[768,768]{1,0:T(8,128)S(1)} %copy-done.4, f32[2,768,768]{2,1,0:T(8,128)S(1)} %fusion.2), kind=kOutput, calls=%fused_computation.4 | convolution fusion | flops 10876354560 | bytes 11796488 | tf_op jit(solution)/shard_map/kij,kjl->kil/dot_general | solution.py:52
  327.2 12.1 %fusion.40 = f32[2,768,768]{2,1,0:T(8,128)S(1)} fusion(f32[2,768,768]{2,1,0:T(8,128)S(1)} %bitcast.80, f32[2,768,768]{2,1,0:T(8,128)S(1)} %multiply_subtract_fusion.2), kind=kOutput, calls=%fused_computation.65 | convolution fusion | flops 10871635968 | bytes 14155776 | tf_op jit(solution)/shard_map/kij,kjl->kil/dot_general | solution.py:51
  339.3 12.7 %multiply_subtract_fusion.1 = f32[2,768,768]{2,1,0:T(8,128)S(1)} fusion(f32[2,768,768]{2,1,0:T(8,128)S(1)} %multiply_subtract_fusion.2, f32[2,768,768]{2,1,0:T(8,128)S(1)} %fusion.40), kind=kOutput, calls=%fused_computation.3 | convolution fusion | flops 10873995264 | bytes 14155776 | tf_op jit(solution)/shard_map/kij,kjl->kil/dot_general | solution.py:52
  352.0 12.3 %fusion.41 = f32[2,768,768]{2,1,0:T(8,128)S(1)} fusion(f32[2,768,768]{2,1,0:T(8,128)S(1)} %bitcast.80, f32[2,768,768]{2,1,0:T(8,128)S(1)} %multiply_subtract_fusion.1), kind=kOutput, calls=%fused_computation.66 | convolution fusion | flops 10871635968 | bytes 14155776 | tf_op jit(solution)/shard_map/kij,kjl->kil/dot_general | solution.py:51
  364.3 12.5 %multiply_subtract_fusion = f32[2,768,768]{2,1,0:T(8,128)S(1)} fusion(f32[2,768,768]{2,1,0:T(8,128)S(1)} %multiply_subtract_fusion.1, f32[2,768,768]{2,1,0:T(8,128)S(1)} %fusion.41), kind=kOutput, calls=%fused_computation.2 | convolution fusion | flops 10873995264 | bytes 14155776 | tf_op jit(solution)/shard_map/kij,kjl->kil/dot_general | solution.py:52
  376.8 2.6 slice_select_fusion
  381.1 1.9 constant_dynamic-slice_fusion
  383.1 89.3 %all-reduce.4.cloned.1.call-done = (f32[1,768,768]{2,1,0:T(8,128)}, f32[1,768,768]{2,1,0:T(8,128)}) async-done(((f32[1,768,768]{2,1,0:T(8,128)}, f32[1,768,768]{2,1,0:T(8,128)}), (f32[1,768,768]{2,1,0:T(8,128)}, f32[1,768,768]{2,1,0:T(8,128)})) %all-reduce.4.cloned.1.call-update) | async-done | bytes 4718608 | tf_op jit(solution)/shard_map/psum | solution.py:14
  472.4 2.1 fusion.8
  474.5 14.5 %all-gather.5.cloned.1.call-done = bf16[6,768,768]{2,1,0:T(8,128)(2,1)} async-done(((bf16[6,96,768]{2,1,0:T(8,128)(2,1)}), bf16[6,768,768]{2,1,0:T(8,128)(2,1)}) %all-gather.5.cloned.1.call-update) | async-done | bytes 7077904 | tf_op jit(solution)/shard_map/all_gather | solution.py:61
  489.0 23.5 %all-gather.3.cloned.1.call-done = f32[8,96,768]{2,1,0:T(8,128)} async-done(((f32[2,96,768]{2,1,0:T(8,128)}), f32[8,96,768]{2,1,0:T(8,128)}) %all-gather.3.cloned.1.call-update) | async-done | bytes 2359312 | tf_op jit(solution)/shard_map/all_gather | solution.py:54
  512.5 6.7 %fusion.42 = f32[6,96,768]{2,1,0:T(8,128)S(1)} fusion(f32[8,96,768]{2,1,0:T(8,128)} %all-gather.3.cloned.1.call-done, bf16[6,768,768]{2,1,0:T(8,128)(2,1)} %all-gather.5.cloned.1.call-done), kind=kOutput, calls=%fused_computation.67 | convolution fusion | flops 4076863488 | bytes 11206656 | tf_op jit(solution)/shard_map/wrn,wnd->wrd/dot_general | solution.py:63
  (39 shorter events, 9.1 us)
Async XLA Ops:
  7.4 1.0 copy-start
  7.4 7.6 %copy-start.7 = (bf16[5,256,768]{2,1,0:T(8,128)(2,1)S(1)}, bf16[5,256,768]{2,1,0:T(8,128)(2,1)}, u32[]{:S(2)}) copy-start(bf16[5,256,768]{2,1,0:T(8,128)(2,1)} %param.7) | copy-start | bytes 5898244
  7.4 96.8 %reduce-scatter.2.cloned.1.call-start = ((), (), s32[]{:S(2)}) async-start(), calls=%async_computation.1 | async-start | bytes 11796480 | tf_op jit(solution)/shard_map/reduce_scatter | solution.py:37
  12.3 8.9 %copy-start.6 = (bf16[32,768]{1,0:T(8,128)(2,1)S(1)}, bf16[32,768]{1,0:T(8,128)(2,1)}, u32[]{:S(2)}) copy-start(bf16[32,768]{1,0:T(8,128)(2,1)} %param.9) | copy-start | bytes 147460
  22.9 449.5 %all-reduce.4.cloned.1.call-start = ((), (), s32[]{:S(2)}) async-start(), calls=%async_computation.4 | async-start | bytes 9437184 | tf_op jit(solution)/shard_map/psum | solution.py:14
  291.9 3.8 copy-start.2
  298.7 15.6 %copy-start.4 = (f32[768,768]{1,0:T(8,128)S(1)}, f32[768,768]{1,0:T(8,128)}, u32[]{:S(2)}) copy-start(f32[768,768]{1,0:T(8,128)} %fusion.26) | copy-start | bytes 7077892
  298.7 28.4 %slice-start = ((s8[4718592]{0:T(1024)(128)(4,1)}), s8[4194304]{0:T(1024)(128)(4,1)S(1)}, s32[]{:S(2)}) async-start(s8[4718592]{0:T(1024)(128)(4,1)} %bitcast.79), calls=%async_computation.5 | async-start | bytes 8388608
  314.3 12.9 %slice-start.1 = ((s8[4718592]{0:T(1024)(128)(4,1)}), s8[524288]{0:T(1024)(128)(4,1)S(1)}, s32[]{:S(2)}) async-start(s8[4718592]{0:T(1024)(128)(4,1)} %bitcast.79), calls=%async_computation.6 | async-start | bytes 1048576
  376.8 3.6 copy-start.3
  380.5 108.5 %all-gather.5.cloned.1.call-start = ((), (), s32[]{:S(2)}) async-start(), calls=%async_computation.3 | async-start | bytes 7962624 | tf_op jit(solution)/shard_map/all_gather | solution.py:61
  381.1 131.4 %all-gather.3.cloned.1.call-start = ((), (), s32[]{:S(2)}) async-start(), calls=%async_computation.2 | async-start | bytes 2949120 | tf_op jit(solution)/shard_map/all_gather | solution.py:54
  474.5 46.7 %copy-start.5 = (f32[6,96,192]{2,1,0:T(8,128)S(1)}, f32[6,96,192]{2,1,0:T(8,128)}, u32[]{:S(2)}) copy-start(f32[6,96,192]{2,1,0:T(8,128)} %param.11) | copy-start | bytes 1327108
  512.5 9.5 %copy-start.1 = (bf16[256,768]{1,0:T(8,128)(2,1)S(1)}, bf16[256,768]{1,0:T(8,128)(2,1)}, u32[]{:S(2)}) copy-start(bf16[256,768]{1,0:T(8,128)(2,1)} %param.6) | copy-start | bytes 1179652
Sparse Core Ops, SparseCore 0:
  23.0 81.1 reduce-scatter.1
  380.6 91.7 all-reduce.3
Sparse Core Ops, SparseCore 1:
  383.2 105.8 all-gather.4
  490.4 22.1 all-gather.2
where the time goes:
time: 534 us; the launch traced here: 530 us
  waiting for transfers between devices  207 us (39%)
  blocking collectives  188 us (35%)
  matrix products  101 us (19%)
  between operations  15.3 us (3%)
  other arithmetic  14.3 us (3%)
    psum x1, blocking collectives, on_device(): factor_full = lax.psum(summed, 'shard')  188 us
    psum x1, waiting for transfers between devices, broadcast(): return lax.psum(jnp.where(mine, array, jnp.zeros_like(array)), axis)  89.3 us
    reduce_scatter x1, waiting for transfers between devices, on_device(): lax.psum_scatter(stacked, 'group', scatter_dimension=0, tiled=True)  79.3 us
    dot_general x3, matrix products, on_device(): product = jnp.einsum('kij,kjl->kil', matrix, approx, precision=PRECISE)  39.9 us
    dot_general x3, matrix products, on_device(): jnp.einsum('kij,kjl->kil', approx, product, precision=PRECISE)  38.1 us
    all_gather x1, waiting for transfers between devices, on_device(): all_rows = lax.all_gather(own_rows, 'group', axis=0, tiled=True)  23.5 us
    all_gather x1, waiting for transfers between devices, on_device(): gathered = lax.all_gather(weight_grads, 'shard', axis=1, tiled=True)  14.5 us
    dot_general x8, matrix products, outer_sum(): lax.dot_general(matrix_rows, matrix_rows, (((0,), (0,)), ((), ())), prefe...  14.5 us
  transfers between devices with their start and end apart: 4, of which 4 were waited for; matrix products, arithmetic and copies ran while one was open for 1% of the time, Pallas kernels for 0%

commit v1 on v0

--- a/solution.py
+++ b/solution.py
@@ -2,11 +2,36 @@
 import jax.numpy as jnp
 from jax import lax
 from jax.sharding import PartitionSpec as P
+from jax.lax import axis_index, axis_size, ppermute
 
 ITERS = 3
 PRECISE = lax.Precision.HIGHEST
 DAMPING = 0.1
 MOMENTUM = 0.9
+
+
+def _watch_leaf(w_in, array_axis):
+    built = list(w_in.shape[1:])
+    built[array_axis] *= w_in.shape[0]
+    return jnp.moveaxis(w_in, 0, array_axis).reshape(built)
+
+
+def proceed_halves(inputs, net_axis, which_dim):
+    count_all = axis_size(net_axis)
+    rows = [(b, (b + 1) % count_all) for b in range(count_all)]
+    leaves = [(kk, w) for w, kk in rows]
+    even, part_next = ([], [])
+    j0 = 0
+    while j0 < count_all - 1:
+        if j0 % 2 == 0:
+            even.append(ppermute(even[-1] if even else inputs, perm=rows, axis_name=net_axis))
+        else:
+            part_next.append(ppermute(part_next[-1] if part_next else inputs, net_axis, leaves))
+        j0 += 1
+    prior = jnp.stack([*even[::-1], inputs, *part_next], 0)
+    plain = axis_index(net_axis) - len(even)
+    prior = prior[(jnp.arange(count_all) - plain) % count_all]
+    return _watch_leaf(prior, which_dim)
 
 
 def broadcast(array, axis, root):
@@ -58,7 +83,7 @@
     input_cols = lax.dynamic_slice_in_dim(input_inv, group_pos * col_block, col_block, 2)
     out_inverse = all_rows[2:8]
     initial = jnp.zeros(out_inverse.shape, jnp.float32)
-    gathered = lax.all_gather(weight_grads, "shard", axis=1, tiled=True)
+    gathered = proceed_halves(weight_grads, "shard", 1)
     columns = lax.slice_in_dim(out_inverse, 0, gathered.shape[1], axis=2)
     left_side = initial + jnp.einsum(
         "wrn,wnd->wrd", columns, gathered.astype(jnp.float32), precision=PRECISE

time: 534 us -> 571 us (1.069)
  local copies, waits for them, and re-layouts: 4.07 us -> 31.1 us
  starting transfers between devices: 0.13 us -> 14.3 us
    ppermute x0 -> x7, waiting for transfers between devices: none -> 125 us  [the longest x4 125 us: proceed_halves(): ppermute(even[-1] if even else inputs, perm=rows, axis_name=net_axis)]
    psum x1, waiting for transfers between devices: 89.3 us -> 0.01 us  [broadcast(): return lax.psum(jnp.where(mine, array, jnp.zeros_like(array)), axis)]
    all_gather x1, waiting for transfers between devices: 23.5 us -> 0.02 us  [on_device(): all_rows = lax.all_gather(own_rows, 'group', axis=0, tiled=True)]
    all_gather x1 -> x0, waiting for transfers between devices: 14.5 us -> none  [on_device(): gathered = lax.all_gather(weight_grads, 'shard', axis=1, tiled=True)]
    ppermute x0 -> x7, starting transfers between devices: none -> 14.2 us  [the longest x3 9.11 us: proceed_halves(): ppermute(part_next[-1] if part_next else inputs, net_axis, leaves)]
    unnamed x20 -> x29, local copies, waits for them, and re-layouts: 2.14 us -> 14.7 us
    gather x0 -> x1, local copies, waits for them, and re-layouts: none -> 6.94 us  [proceed_halves(): prior = prior[(jnp.arange(count_all) - plain) % count_all]]
    transpose x0 -> x1, local copies, waits for them, and re-layouts: none -> 6.48 us  [_watch_leaf(): return jnp.moveaxis(w_in, 0, array_axis).reshape(built)]
  transfers between devices with their start and end apart: 4 -> 10, of which waited for: 4 -> 6; matrix products, arithmetic and copies ran while one was open for 1% -> 6% of each run, Pallas kernels for 0% -> 0%
where the time goes in v1:
time: 571 us; the launch traced here: 567 us
  waiting for transfers between devices  204 us (36%)
  blocking collectives  188 us (33%)
  matrix products  101 us (18%)
  local copies, waits for them, and re-layouts  31.1 us (5%)
  other arithmetic  14.4 us (3%)
  starting transfers between devices  14.3 us (3%)
  between operations  13.6 us (2%)
    psum x1, blocking collectives, on_device(): factor_full = lax.psum(summed, 'shard')  188 us
    ppermute x4, waiting for transfers between devices, proceed_halves(): ppermute(even[-1] if even else inputs, perm=rows, axis_name=net_axis)  125 us
    reduce_scatter x1, waiting for transfers between devices, on_device(): lax.psum_scatter(stacked, 'group', scatter_dimension=0, tiled=True)  79.3 us
    dot_general x3, matrix products, on_device(): product = jnp.einsum('kij,kjl->kil', matrix, approx, precision=PRECISE)  39.9 us
    dot_general x3, matrix products, on_device(): jnp.einsum('kij,kjl->kil', approx, product, precision=PRECISE)  38.1 us
    unnamed x29, local copies, waits for them, and re-layouts  14.7 us
    dot_general x8, matrix products, outer_sum(): lax.dot_general(matrix_rows, matrix_rows, (((0,), (0,)), ((), ())), prefe...  14.4 us
  transfers between devices with their start and end apart: 10, of which 6 were waited for; matrix products, arithmetic and copies ran while one was open for 6% of the time, Pallas kernels for 0%

profile of v1, /device:TPU:0, one launch (start us, length us, event | category | flops | bytes accessed | tf_op | source)
XLA Modules:
  0.0 566.6 jit_solution(3289695033950375229)
XLA Ops:
  9.1 2.4 fusion.10
  11.5 2.7 fusion.16
  24.0 79.3 %reduce-scatter.2.cloned.1.call-done = bf16[2,768,768]{2,1,0:T(8,128)(2,1)} async-done(((bf16[8,768,768]{2,1,0:T(8,128)(2,1)}), bf16[2,768,768]{2,1,0:T(8,128)(2,1)}) %reduce-scatter.2.cloned.1.call-update) | async-done | bytes 2359312 | tf_op jit(solution)/shard_map/reduce_scatter | solution.py:62
  103.3 187.8 %all-reduce.5 = f32[2,768,768]{2,1,0:T(8,128)} all-reduce(bf16[2,768,768]{2,1,0:T(8,128)(2,1)} %reduce-scatter.2.cloned.1.call-done), channel_id=1, replica_groups=mesh['group'=4,'shard'=8] {'shard'}, use_global_device_ids=true, to_apply=%region_1.2 | all-reduce | flops 1179648 | bytes 7077888 | tf_op jit(solution)/shard_map/psum | solution.py:68
  291.0 3.7 select_reduce_fusion
  294.8 3.0 abs_reduce_fusion
  297.9 15.5 %fusion.2 = f32[2,768,768]{2,1,0:T(8,128)S(1)} fusion(f32[2,768,768]{2,1,0:T(8,128)} %get-tuple-element.8, f32[2]{0:T(128)S(1)} %reduce_max.9, f32[768,768]{1,0:T(8,128)} %fusion.26), kind=kOutput, calls=%fused_computation.11 | convolution fusion | flops 10872815616 | bytes 11796488 | tf_op jit(solution)/shard_map/kij,kjl->kil/dot_general | solution.py:76
  313.4 12.8 %multiply_subtract_fusion.2 = f32[2,768,768]{2,1,0:T(8,128)S(1)} fusion(f32[2]{0:T(128)S(1)} %reduce_max.9, f32[768,768]{1,0:T(8,128)S(1)} %copy-done.4, f32[2,768,768]{2,1,0:T(8,128)S(1)} %fusion.2), kind=kOutput, calls=%fused_computation.5 | convolution fusion | flops 10876354560 | bytes 11796488 | tf_op jit(solution)/shard_map/kij,kjl->kil/dot_general | solution.py:77
  326.3 12.1 %fusion.42 = f32[2,768,768]{2,1,0:T(8,128)S(1)} fusion(f32[2,768,768]{2,1,0:T(8,128)S(1)} %bitcast.100, f32[2,768,768]{2,1,0:T(8,128)S(1)} %multiply_subtract_fusion.2), kind=kOutput, calls=%fused_computation.81 | convolution fusion | flops 10871635968 | bytes 14155776 | tf_op jit(solution)/shard_map/kij,kjl->kil/dot_general | solution.py:76
  338.4 12.7 %multiply_subtract_fusion.1 = f32[2,768,768]{2,1,0:T(8,128)S(1)} fusion(f32[2,768,768]{2,1,0:T(8,128)S(1)} %multiply_subtract_fusion.2, f32[2,768,768]{2,1,0:T(8,128)S(1)} %fusion.42), kind=kOutput, calls=%fused_computation.4 | convolution fusion | flops 10873995264 | bytes 14155776 | tf_op jit(solution)/shard_map/kij,kjl->kil/dot_general | solution.py:77
  351.1 12.3 %fusion.43 = f32[2,768,768]{2,1,0:T(8,128)S(1)} fusion(f32[2,768,768]{2,1,0:T(8,128)S(1)} %bitcast.100, f32[2,768,768]{2,1,0:T(8,128)S(1)} %multiply_subtract_fusion.1), kind=kOutput, calls=%fused_computation.82 | convolution fusion | flops 10871635968 | bytes 14155776 | tf_op jit(solution)/shard_map/kij,kjl->kil/dot_general | solution.py:76
  363.4 12.5 %multiply_subtract_fusion = f32[2,768,768]{2,1,0:T(8,128)S(1)} fusion(f32[2,768,768]{2,1,0:T(8,128)S(1)} %multiply_subtract_fusion.1, f32[2,768,768]{2,1,0:T(8,128)S(1)} %fusion.43), kind=kOutput, calls=%fused_computation.3 | convolution fusion | flops 10873995264 | bytes 14155776 | tf_op jit(solution)/shard_map/kij,kjl->kil/dot_general | solution.py:77
  375.9 2.7 slice_select_fusion
  380.8 23.7 %collective-permute-done = bf16[6,96,768]{2,1,0:T(8,128)(2,1)S(1)} collective-permute-done((bf16[6,96,768]{2,1,0:T(8,128)(2,1)S(1)}, bf16[6,96,768]{2,1,0:T(8,128)(2,1)S(1)}, u32[]{:S(2)}, u32[]{:S(2)}) %collective-permute-start) | collective-permute-done | bytes 884768 | tf_op jit(solution)/shard_map/ppermute | solution.py:27
  404.5 4.7 collective-permute-start.4
  409.3 31.7 %collective-permute-done.1 = bf16[6,96,768]{2,1,0:T(8,128)(2,1)} collective-permute-done((bf16[6,96,768]{2,1,0:T(8,128)(2,1)S(1)}, bf16[6,96,768]{2,1,0:T(8,128)(2,1)}, u32[]{:S(2)}, u32[]{:S(2)}) %collective-permute-start.1) | collective-permute-done | bytes 884768 | tf_op jit(solution)/shard_map/ppermute | solution.py:27
  440.9 2.6 collective-permute-start.2
  447.7 34.2 %collective-permute-done.2 = bf16[6,96,768]{2,1,0:T(8,128)(2,1)} collective-permute-done((bf16[6,96,768]{2,1,0:T(8,128)(2,1)}, bf16[6,96,768]{2,1,0:T(8,128)(2,1)}, u32[]{:S(2)}, u32[]{:S(2)}) %collective-permute-start.2) | collective-permute-done | bytes 884768 | tf_op jit(solution)/shard_map/ppermute | solution.py:27
  481.9 2.5 collective-permute-start.3
  484.5 2.2 collective-permute-start.6
  486.7 35.2 %collective-permute-done.3 = bf16[6,96,768]{2,1,0:T(8,128)(2,1)} collective-permute-done((bf16[6,96,768]{2,1,0:T(8,128)(2,1)}, bf16[6,96,768]{2,1,0:T(8,128)(2,1)}, u32[]{:S(2)}, u32[]{:S(2)}) %collective-permute-start.3) | collective-permute-done | bytes 884768 | tf_op jit(solution)/shard_map/ppermute | solution.py:27
  534.4 6.9 %gather_fusion = bf16[8,6,96,768]{3,2,1,0:T(8,128)(2,1)} fusion(bf16[8,6,96,768]{3,2,1,0:T(8,128)(2,1)} %bitcast_dynamic-update-slice_fusion, s32[1024]{0:T(1024)S(1)} %pad_clamp_fusion), kind=kCustom, calls=%fused_computation | custom fusion | bytes 14155808 | tf_op jit(solution)/shard_map/gather | solution.py:33
  541.4 6.5 %copy.13 = bf16[6,8,96,768]{3,2,1,0:T(8,128)(2,1)} copy(bf16[6,8,96,768]{3,2,0,1:T(8,128)(2,1)} %bitcast.101) | data formatting | bytes 14155776 | tf_op jit(solution)/shard_map/transpose | solution.py:16
  550.0 7.0 %fusion.44 = f32[6,96,768]{2,1,0:T(8,128)S(1)} fusion(f32[8,96,768]{2,1,0:T(8,128)} %all-gather.2.cloned.1.call-done, bf16[6,768,768]{2,1,0:T(8,128)(2,1)} %bitcast.102), kind=kOutput, calls=%fused_computation.83 | convolution fusion | flops 4076863488 | bytes 11206656 | tf_op jit(solution)/shard_map/wrn,wnd->wrd/dot_general | solution.py:88
  (64 shorter events, 36.4 us)
Async XLA Ops:
  6.5 1.0 copy-start
  6.5 7.6 %copy-start.8 = (bf16[5,256,768]{2,1,0:T(8,128)(2,1)S(1)}, bf16[5,256,768]{2,1,0:T(8,128)(2,1)}, u32[]{:S(2)}) copy-start(bf16[5,256,768]{2,1,0:T(8,128)(2,1)} %param.7) | copy-start | bytes 5898244
  6.5 96.7 %reduce-scatter.2.cloned.1.call-start = ((), (), s32[]{:S(2)}) async-start(), calls=%async_computation.1 | async-start | bytes 11796480 | tf_op jit(solution)/shard_map/reduce_scatter | solution.py:62
  11.5 8.9 %copy-start.7 = (bf16[32,768]{1,0:T(8,128)(2,1)S(1)}, bf16[32,768]{1,0:T(8,128)(2,1)}, u32[]{:S(2)}) copy-start(bf16[32,768]{1,0:T(8,128)(2,1)} %param.9) | copy-start | bytes 147460
  22.0 525.9 %all-reduce.4.cloned.1.call-start = ((), (), s32[]{:S(2)}) async-start(), calls=%async_computation.3 | async-start | bytes 9437184 | tf_op jit(solution)/shard_map/psum | solution.py:39
  291.0 3.8 copy-start.2
  297.9 15.5 %copy-start.4 = (f32[768,768]{1,0:T(8,128)S(1)}, f32[768,768]{1,0:T(8,128)}, u32[]{:S(2)}) copy-start(f32[768,768]{1,0:T(8,128)} %fusion.26) | copy-start | bytes 7077892
  297.9 28.4 %slice-start = ((s8[4718592]{0:T(1024)(128)(4,1)}), s8[4194304]{0:T(1024)(128)(4,1)S(1)}, s32[]{:S(2)}) async-start(s8[4718592]{0:T(1024)(128)(4,1)} %bitcast.99), calls=%async_computation.4 | async-start | bytes 8388608
  313.4 12.9 %slice-start.1 = ((s8[4718592]{0:T(1024)(128)(4,1)}), s8[524288]{0:T(1024)(128)(4,1)S(1)}, s32[]{:S(2)}) async-start(s8[4718592]{0:T(1024)(128)(4,1)} %bitcast.99), calls=%async_computation.5 | async-start | bytes 1048576
  375.9 3.7 copy-start.3
  379.6 1.2 copy-start.5
  379.6 170.3 %all-gather.2.cloned.1.call-start = ((), (), s32[]{:S(2)}) async-start(), calls=%async_computation.2 | async-start | bytes 2949120 | tf_op jit(solution)/shard_map/all_gather | solution.py:79
  380.8 23.7 %collective-permute-start = (bf16[6,96,768]{2,1,0:T(8,128)(2,1)S(1)}, bf16[6,96,768]{2,1,0:T(8,128)(2,1)S(1)}, u32[]{:S(2)}, u32[]{:S(2)}) collective-permute-start(bf16[6,96,768]{2,1,0:T(8,128)(2,1)S(1)} %copy-done.5), channel_id=1, source_target_pairs={{0,1},{1,2},{2,3},{3,4},{4,5},{5,6},{6,7},{7,0},{8,9},{9,10},{10,1... | collective-permute-start | bytes 2654216 | tf_op jit(solution)/shard_map/ppermute | solution.py:27
  404.5 36.4 %collective-permute-start.1 = (bf16[6,96,768]{2,1,0:T(8,128)(2,1)S(1)}, bf16[6,96,768]{2,1,0:T(8,128)(2,1)}, u32[]{:S(2)}, u32[]{:S(2)}) collective-permute-start(bf16[6,96,768]{2,1,0:T(8,128)(2,1)S(1)} %collective-permute-done), channel_id=1, source_target_pairs={{0,1},{1,2},{2,3},{3,4},{4,5},{5,6},{6,7},{7,0},{8,9},{9,10},{10,1... | collective-permute-start | bytes 2654216 | tf_op jit(solution)/shard_map/ppermute | solution.py:27
  404.5 40.9 %collective-permute-start.4 = (bf16[6,96,768]{2,1,0:T(8,128)(2,1)S(1)}, bf16[6,96,768]{2,1,0:T(8,128)(2,1)S(1)}, u32[]{:S(2)}, u32[]{:S(2)}) collective-permute-start(bf16[6,96,768]{2,1,0:T(8,128)(2,1)S(1)} %copy-done.5), channel_id=1, source_target_pairs={{1,0},{2,1},{3,2},{4,3},{5,4},{6,5},{7,6},{0,7},{9,8},{10,9},{11,1... | collective-permute-start | bytes 2654216 | tf_op jit(solution)/shard_map/ppermute | solution.py:29
  440.9 41.0 %collective-permute-start.2 = (bf16[6,96,768]{2,1,0:T(8,128)(2,1)}, bf16[6,96,768]{2,1,0:T(8,128)(2,1)}, u32[]{:S(2)}, u32[]{:S(2)}) collective-permute-start(bf16[6,96,768]{2,1,0:T(8,128)(2,1)} %collective-permute-done.1), channel_id=1, source_target_pairs={{0,1},{1,2},{2,3},{3,4},{4,5},{5,6},{6,7},{7,0},{8,9},{9,10},{10,1... | collective-permute-start | bytes 2654216 | tf_op jit(solution)/shard_map/ppermute | solution.py:27
  445.5 39.0 %collective-permute-start.5 = (bf16[6,96,768]{2,1,0:T(8,128)(2,1)S(1)}, bf16[6,96,768]{2,1,0:T(8,128)(2,1)}, u32[]{:S(2)}, u32[]{:S(2)}) collective-permute-start(bf16[6,96,768]{2,1,0:T(8,128)(2,1)S(1)} %collective-permute-done.4), channel_id=1, source_target_pairs={{1,0},{2,1},{3,2},{4,3},{5,4},{6,5},{7,6},{0,7},{9,8},{10,9},{11,1... | collective-permute-start | bytes 2654216 | tf_op jit(solution)/shard_map/ppermute | solution.py:29
  481.9 40.0 %collective-permute-start.3 = (bf16[6,96,768]{2,1,0:T(8,128)(2,1)}, bf16[6,96,768]{2,1,0:T(8,128)(2,1)}, u32[]{:S(2)}, u32[]{:S(2)}) collective-permute-start(bf16[6,96,768]{2,1,0:T(8,128)(2,1)} %collective-permute-done.2), channel_id=1, source_target_pairs={{0,1},{1,2},{2,3},{3,4},{4,5},{5,6},{6,7},{7,0},{8,9},{9,10},{10,1... | collective-permute-start | bytes 2654216 | tf_op jit(solution)/shard_map/ppermute | solution.py:27
  484.5 49.0 %collective-permute-start.6 = (bf16[6,96,768]{2,1,0:T(8,128)(2,1)}, bf16[6,96,768]{2,1,0:T(8,128)(2,1)S(1)}, u32[]{:S(2)}, u32[]{:S(2)}) collective-permute-start(bf16[6,96,768]{2,1,0:T(8,128)(2,1)} %collective-permute-done.5), channel_id=1, source_target_pairs={{1,0},{2,1},{3,2},{4,3},{5,4},{6,5},{7,6},{0,7},{9,8},{10,9},{11,1... | collective-permute-start | bytes 2654216 | tf_op jit(solution)/shard_map/ppermute | solution.py:29
  550.0 8.9 %copy-start.6 = (f32[6,96,192]{2,1,0:T(8,128)S(1)}, f32[6,96,192]{2,1,0:T(8,128)}, u32[]{:S(2)}) copy-start(f32[6,96,192]{2,1,0:T(8,128)} %param.11) | copy-start | bytes 1327108
  550.0 9.8 %copy-start.1 = (bf16[256,768]{1,0:T(8,128)(2,1)S(1)}, bf16[256,768]{1,0:T(8,128)(2,1)}, u32[]{:S(2)}) copy-start(bf16[256,768]{1,0:T(8,128)(2,1)} %param.6) | copy-start | bytes 1179652
Sparse Core Ops, SparseCore 0:
  22.1 81.1 reduce-scatter.1
  379.8 91.6 all-reduce.3
  473.1 24.2 all-gather.1
